TPU v7x, 256 devices: a whole 4x4x8 slice. The times are simulated.
256 devices in a mesh: ctx: 64 (over z, y, x_lo), head: 4 (over x_hi, core).
Axes of the slice: x: 4 (x_hi: 2, x_lo: 2; x = x_hi * 2 + x_lo), y: 4, z: 8, core: 2. Of those that a mesh axis runs over, the one named last changes fastest.
Arguments:
- q_nope: bfloat16 [8192, 64, 128], P('ctx', 'head'), may hold values from -6 to 6
- q_rope: bfloat16 [8192, 4096], P('ctx', 'head'), may hold values from -80 to 80
- latent: bfloat16 [8192, 576], P('ctx'), may hold values from -4 to 4
- positions: int32 [8192], P('ctx'), may hold values from 0 to 8191, each once
- w_uk: bfloat16 [64, 128, 512], P('head'), may hold values from -0.5 to 0.5
- w_uv: bfloat16 [64, 512, 128], P('head'), may hold values from -0.25 to 0.25
- w_o: bfloat16 [8192, 3584], P('head', 'ctx'), may hold values from -0.5 to 0.5
Outputs:
- projected: bfloat16 [8192, 3584], P(('ctx', 'head'))
Inputs may be any that keep to these rules, and one draw needn't show every extreme that they name: positions holds each of 0 to 8191 once.
All inputs are finite; a program needn't handle non-finite values.
Results may differ from a plain program's by a relative error of at most 0.015.
Values may be sent and summed in bfloat16 or wider, within the bound.
No kernel may reach another device: no remote copies, remote signals or barrier semaphores. Data moves between devices by JAX's collectives and lax.ppermute only.
A program may use at most 128 MiB of HBM per device.

v0:
```python
import jax
import jax.numpy as jnp
from jax import lax
from jax.sharding import PartitionSpec as P


def from_behind(x, axis, by):
    count = lax.axis_size(axis)
    return lax.ppermute(x, axis, [(i, (i + by) % count) for i in range(count)])


def local(q_nope, q_rope, latent, positions, w_uk, w_uv, w_o):
    tok_rows, heads, nope_dim = q_nope.shape
    lat_dim = w_uk.shape[2]
    rope_dim = q_rope.shape[1] // heads
    scale = (nope_dim + rope_dim) ** (-0.5)
    steps = lax.axis_size("ctx") // 4
    q_latent = jnp.einsum("thn,hnl->thl", q_nope, w_uk, preferred_element_type=jnp.float32).astype(
        jnp.bfloat16
    )
    q_rot = q_rope.reshape(tok_rows, heads, rope_dim)

    def absorb(state, keys, key_pos):
        running, total, summed = state
        scores = jnp.einsum(
            "thl,kl->thk", q_latent, keys[:, :lat_dim], preferred_element_type=jnp.float32
        )
        scores = scores + jnp.einsum(
            "thr,kr->thk", q_rot, keys[:, lat_dim:], preferred_element_type=jnp.float32
        )
        scores = scores * scale
        visible = key_pos[None, None, :] <= positions[:, None, None]
        scores = jnp.where(visible, scores, -jnp.inf)
        newest = jnp.maximum(running, jnp.max(scores, axis=-1))
        factor = jnp.exp(running - newest)
        weights = jnp.exp(scores - newest[:, :, None])
        total = total * factor + jnp.sum(weights, axis=-1)
        summed = summed * factor[:, :, None] + jnp.einsum(
            "thk,kl->thl",
            weights.astype(jnp.bfloat16),
            keys[:, :lat_dim],
            preferred_element_type=jnp.float32,
        )
        return (newest, total, summed)

    start_state = (
        jnp.full((tok_rows, heads), -jnp.inf, jnp.float32),
        jnp.zeros((tok_rows, heads), jnp.float32),
        jnp.zeros((tok_rows, heads, lat_dim), jnp.float32),
    )
    state = absorb(start_state, latent, positions)

    def turn(carry, unused):
        current, block, block_pos = carry
        block, block_pos = from_behind((block, block_pos), "ctx", 1)
        current = absorb(current, block, block_pos)
        return ((current, block, block_pos), None)

    carried, unused = lax.scan(turn, (state, latent, positions), None, length=steps - 1)
    state = carried[0]
    running, total, summed = state
    o_latent = (summed / total[:, :, None]).astype(jnp.bfloat16)
    head_out = jnp.einsum(
        "thl,hlv->thv", o_latent, w_uv, preferred_element_type=jnp.float32
    ).astype(jnp.bfloat16)
    head_out = head_out.reshape(tok_rows, heads * w_uv.shape[2])
    product = lax.dot_general(
        lax.all_gather(w_o, "ctx", axis=1, tiled=True),
        head_out,
        (((0,), (1,)), ((), ())),
        preferred_element_type=jnp.float32,
    )
    columns_first = product.astype(jnp.bfloat16)
    partial_out = columns_first.T
    summed_out = lax.psum_scatter(
        partial_out.astype(jnp.float32).astype(jnp.bfloat16),
        "head",
        scatter_dimension=0,
        tiled=True,
    )
    return summed_out


def solution(mesh):
    placed = (
        P("ctx", "head", None),
        P("ctx", "head"),
        P("ctx", None),
        P("ctx"),
        P("head", None, None),
        P("head", None, None),
        P("head", "ctx"),
    )
    return jax.shard_map(
        local, mesh=mesh, in_specs=placed, out_specs=P(("ctx", "head"), None), check_vma=False
    )
```

profile of v0, /device:TPU:1, one launch (start us, length us, event | category | flops | bytes accessed | tf_op | source)
XLA Modules:
  0.0 448.3 jit_solution(5801382140468540568)
XLA Ops:
  9.5 3.1 convert_bitcast_fusion
  12.7 3.9 copy.17
  20.0 2.7 convolution_add_fusion.1
  22.8 302.1 %while.18 = (s32[]{:T(128)}, f32[128,16]{0,1:T(8,128)S(1)}, f32[128,16]{0,1:T(8,128)S(1)}, f32[128,16,512]{2,0,1:T(8,128)}, bf16[128,576]{1,0:T(8,128)(2,1)S(1)}...) while((s32[]{:T(128)}, f32[128,16]{0,1:T(8,128)S(1)}, ...), condition=%wide.region_5.6_spmd, body=%wide.region_2.5_spmd.sunk | while | flops 575164416 | bytes 50925804 | solution.py:59
  26.1 7.8 %collective-permute-done = s32[128]{0:T(128)S(1)} collective-permute-done((s32[128]{0:T(128)S(1)}, s32[128]{0:T(128)S(1)}, u32[]{:S(2)}, u32[]{:S(2)}) %collective-permute-start) | collective-permute-done | bytes 544 | tf_op jit(solution)/shard_map/while/body/eval_jaxpr/ppermute | solution.py:9
  34.0 5.1 %collective-permute-done.1 = bf16[128,576]{1,0:T(8,128)(2,1)S(1)} collective-permute-done((bf16[128,576]{1,0:T(8,128)(2,1)S(1)}, bf16[128,576]{1,0:T(8,128)(2,1)S(1)}, u32[]{:S(2)}, u32[]{:S(2)}) %collective-permute-start.1) | collective-permute-done | bytes 147488 | tf_op jit(solution)/shard_map/while/body/eval_jaxpr/ppermute | solution.py:9
  39.4 2.4 select_reduce_fusion.2
  45.8 6.8 %collective-permute-done = s32[128]{0:T(128)S(1)} collective-permute-done((s32[128]{0:T(128)S(1)}, s32[128]{0:T(128)S(1)}, u32[]{:S(2)}, u32[]{:S(2)}) %collective-permute-start) | collective-permute-done | bytes 544 | tf_op jit(solution)/shard_map/while/body/eval_jaxpr/ppermute | solution.py:9
  52.6 5.1 %collective-permute-done.1 = bf16[128,576]{1,0:T(8,128)(2,1)S(1)} collective-permute-done((bf16[128,576]{1,0:T(8,128)(2,1)S(1)}, bf16[128,576]{1,0:T(8,128)(2,1)S(1)}, u32[]{:S(2)}, u32[]{:S(2)}) %collective-permute-start.1) | collective-permute-done | bytes 147488 | tf_op jit(solution)/shard_map/while/body/eval_jaxpr/ppermute | solution.py:9
  58.0 2.4 select_reduce_fusion.2
  64.3 6.6 %collective-permute-done = s32[128]{0:T(128)S(1)} collective-permute-done((s32[128]{0:T(128)S(1)}, s32[128]{0:T(128)S(1)}, u32[]{:S(2)}, u32[]{:S(2)}) %collective-permute-start) | collective-permute-done | bytes 544 | tf_op jit(solution)/shard_map/while/body/eval_jaxpr/ppermute | solution.py:9
  71.1 5.2 %collective-permute-done.1 = bf16[128,576]{1,0:T(8,128)(2,1)S(1)} collective-permute-done((bf16[128,576]{1,0:T(8,128)(2,1)S(1)}, bf16[128,576]{1,0:T(8,128)(2,1)S(1)}, u32[]{:S(2)}, u32[]{:S(2)}) %collective-permute-start.1) | collective-permute-done | bytes 147488 | tf_op jit(solution)/shard_map/while/body/eval_jaxpr/ppermute | solution.py:9
  76.5 2.4 select_reduce_fusion.2
  84.5 5.0 %collective-permute-done = s32[128]{0:T(128)S(1)} collective-permute-done((s32[128]{0:T(128)S(1)}, s32[128]{0:T(128)S(1)}, u32[]{:S(2)}, u32[]{:S(2)}) %collective-permute-start) | collective-permute-done | bytes 544 | tf_op jit(solution)/shard_map/while/body/eval_jaxpr/ppermute | solution.py:9
  89.6 5.7 %collective-permute-done.1 = bf16[128,576]{1,0:T(8,128)(2,1)S(1)} collective-permute-done((bf16[128,576]{1,0:T(8,128)(2,1)S(1)}, bf16[128,576]{1,0:T(8,128)(2,1)S(1)}, u32[]{:S(2)}, u32[]{:S(2)}) %collective-permute-start.1) | collective-permute-done | bytes 147488 | tf_op jit(solution)/shard_map/while/body/eval_jaxpr/ppermute | solution.py:9
  95.6 2.4 select_reduce_fusion.2
  102.0 3.4 collective-permute-start
  105.4 3.2 collective-permute-done
  108.7 7.8 %collective-permute-done.1 = bf16[128,576]{1,0:T(8,128)(2,1)S(1)} collective-permute-done((bf16[128,576]{1,0:T(8,128)(2,1)S(1)}, bf16[128,576]{1,0:T(8,128)(2,1)S(1)}, u32[]{:S(2)}, u32[]{:S(2)}) %collective-permute-start.1) | collective-permute-done | bytes 147488 | tf_op jit(solution)/shard_map/while/body/eval_jaxpr/ppermute | solution.py:9
  116.7 2.4 select_reduce_fusion.2
  123.1 3.0 collective-permute-start
  126.1 3.6 collective-permute-done
  129.8 7.5 %collective-permute-done.1 = bf16[128,576]{1,0:T(8,128)(2,1)S(1)} collective-permute-done((bf16[128,576]{1,0:T(8,128)(2,1)S(1)}, bf16[128,576]{1,0:T(8,128)(2,1)S(1)}, u32[]{:S(2)}, u32[]{:S(2)}) %collective-permute-start.1) | collective-permute-done | bytes 147488 | tf_op jit(solution)/shard_map/while/body/eval_jaxpr/ppermute | solution.py:9
  137.6 2.4 select_reduce_fusion.2
  144.0 2.3 collective-permute-start
  146.3 4.7 %collective-permute-done = s32[128]{0:T(128)S(1)} collective-permute-done((s32[128]{0:T(128)S(1)}, s32[128]{0:T(128)S(1)}, u32[]{:S(2)}, u32[]{:S(2)}) %collective-permute-start) | collective-permute-done | bytes 544 | tf_op jit(solution)/shard_map/while/body/eval_jaxpr/ppermute | solution.py:9
  151.1 6.0 %collective-permute-done.1 = bf16[128,576]{1,0:T(8,128)(2,1)S(1)} collective-permute-done((bf16[128,576]{1,0:T(8,128)(2,1)S(1)}, bf16[128,576]{1,0:T(8,128)(2,1)S(1)}, u32[]{:S(2)}, u32[]{:S(2)}) %collective-permute-start.1) | collective-permute-done | bytes 147488 | tf_op jit(solution)/shard_map/while/body/eval_jaxpr/ppermute | solution.py:9
  157.4 2.4 select_reduce_fusion.2
  163.7 2.8 collective-permute-start
  166.5 4.2 collective-permute-done
  170.8 6.4 %collective-permute-done.1 = bf16[128,576]{1,0:T(8,128)(2,1)S(1)} collective-permute-done((bf16[128,576]{1,0:T(8,128)(2,1)S(1)}, bf16[128,576]{1,0:T(8,128)(2,1)S(1)}, u32[]{:S(2)}, u32[]{:S(2)}) %collective-permute-start.1) | collective-permute-done | bytes 147488 | tf_op jit(solution)/shard_map/while/body/eval_jaxpr/ppermute | solution.py:9
  177.5 2.4 select_reduce_fusion.2
  183.8 3.1 collective-permute-start
  187.0 3.5 collective-permute-done
  190.6 7.6 %collective-permute-done.1 = bf16[128,576]{1,0:T(8,128)(2,1)S(1)} collective-permute-done((bf16[128,576]{1,0:T(8,128)(2,1)S(1)}, bf16[128,576]{1,0:T(8,128)(2,1)S(1)}, u32[]{:S(2)}, u32[]{:S(2)}) %collective-permute-start.1) | collective-permute-done | bytes 147488 | tf_op jit(solution)/shard_map/while/body/eval_jaxpr/ppermute | solution.py:9
  198.4 2.4 select_reduce_fusion.2
  204.8 2.3 collective-permute-start
  207.1 4.3 collective-permute-done
  211.5 5.8 %collective-permute-done.1 = bf16[128,576]{1,0:T(8,128)(2,1)S(1)} collective-permute-done((bf16[128,576]{1,0:T(8,128)(2,1)S(1)}, bf16[128,576]{1,0:T(8,128)(2,1)S(1)}, u32[]{:S(2)}, u32[]{:S(2)}) %collective-permute-start.1) | collective-permute-done | bytes 147488 | tf_op jit(solution)/shard_map/while/body/eval_jaxpr/ppermute | solution.py:9
  217.5 2.4 select_reduce_fusion.2
  223.9 3.2 collective-permute-start
  227.1 3.4 collective-permute-done
  230.6 7.5 %collective-permute-done.1 = bf16[128,576]{1,0:T(8,128)(2,1)S(1)} collective-permute-done((bf16[128,576]{1,0:T(8,128)(2,1)S(1)}, bf16[128,576]{1,0:T(8,128)(2,1)S(1)}, u32[]{:S(2)}, u32[]{:S(2)}) %collective-permute-start.1) | collective-permute-done | bytes 147488 | tf_op jit(solution)/shard_map/while/body/eval_jaxpr/ppermute | solution.py:9
  238.4 2.4 select_reduce_fusion.2
  244.8 2.9 collective-permute-start
  247.7 3.7 collective-permute-done
  251.5 7.4 %collective-permute-done.1 = bf16[128,576]{1,0:T(8,128)(2,1)S(1)} collective-permute-done((bf16[128,576]{1,0:T(8,128)(2,1)S(1)}, bf16[128,576]{1,0:T(8,128)(2,1)S(1)}, u32[]{:S(2)}, u32[]{:S(2)}) %collective-permute-start.1) | collective-permute-done | bytes 147488 | tf_op jit(solution)/shard_map/while/body/eval_jaxpr/ppermute | solution.py:9
  259.2 2.4 select_reduce_fusion.2
  265.5 2.3 collective-permute-start
  267.8 4.3 collective-permute-done
  272.2 6.0 %collective-permute-done.1 = bf16[128,576]{1,0:T(8,128)(2,1)S(1)} collective-permute-done((bf16[128,576]{1,0:T(8,128)(2,1)S(1)}, bf16[128,576]{1,0:T(8,128)(2,1)S(1)}, u32[]{:S(2)}, u32[]{:S(2)}) %collective-permute-start.1) | collective-permute-done | bytes 147488 | tf_op jit(solution)/shard_map/while/body/eval_jaxpr/ppermute | solution.py:9
  278.5 2.4 select_reduce_fusion.2
  284.9 3.2 collective-permute-start
  288.1 3.4 collective-permute-done
  291.6 7.6 %collective-permute-done.1 = bf16[128,576]{1,0:T(8,128)(2,1)S(1)} collective-permute-done((bf16[128,576]{1,0:T(8,128)(2,1)S(1)}, bf16[128,576]{1,0:T(8,128)(2,1)S(1)}, u32[]{:S(2)}, u32[]{:S(2)}) %collective-permute-start.1) | collective-permute-done | bytes 147488 | tf_op jit(solution)/shard_map/while/body/eval_jaxpr/ppermute | solution.py:9
  299.6 2.4 select_reduce_fusion.2
  305.9 2.3 collective-permute-start
  308.2 4.3 collective-permute-done
  312.6 5.6 %collective-permute-done.1 = bf16[128,576]{1,0:T(8,128)(2,1)S(1)} collective-permute-done((bf16[128,576]{1,0:T(8,128)(2,1)S(1)}, bf16[128,576]{1,0:T(8,128)(2,1)S(1)}, u32[]{:S(2)}, u32[]{:S(2)}) %collective-permute-start.1) | collective-permute-done | bytes 147488 | tf_op jit(solution)/shard_map/while/body/eval_jaxpr/ppermute | solution.py:9
  318.5 2.4 select_reduce_fusion.2
  324.8 4.0 fusion.12
  328.8 64.8 %all-gather.2.cloned.1.call-done = bf16[2048,3584]{0,1:T(8,128)(2,1)} async-done(((bf16[2048,56]{0,1:T(8,128)(2,1)}), bf16[2048,3584]{0,1:T(8,128)(2,1)}) %all-gather.2.cloned.1.call-update) | async-done | bytes 14680080 | tf_op jit(solution)/shard_map/all_gather | solution.py:68
  393.7 11.1 %convolution_convert_fusion = bf16[128,3584]{1,0:T(8,128)(2,1)} fusion(bf16[128,2048]{0,1:T(8,128)(2,1)S(1)} %bitcast.44, bf16[2048,3584]{0,1:T(8,128)(2,1)} %all-gather.2.cloned.1.call-done), kind=kOutput, calls=%fused_computation.17 | convolution fusion | flops 1879506944 | bytes 16121856 | tf_op jit(solution)/shard_map/dot_general | solution.py:67
  404.8 36.7 %reduce-scatter.2.cloned.1.call-done = bf16[32,3584]{1,0:T(8,128)(2,1)} async-done(((bf16[128,3584]{1,0:T(8,128)(2,1)}), bf16[32,3584]{1,0:T(8,128)(2,1)}) %reduce-scatter.2.cloned.1.call-update) | async-done | bytes 229392 | tf_op jit(solution)/shard_map/reduce_scatter | solution.py:75
  (230 shorter events, 74.8 us)
Async XLA Ops:
  6.5 3.0 copy-start
  6.5 387.1 %all-gather.2.cloned.1.call-start = ((), (), s32[]{:S(2)}) async-start(), calls=%async_computation.1 | async-start | bytes 14909440 | tf_op jit(solution)/shard_map/all_gather | solution.py:68
  7.3 434.2 %reduce-scatter.2.cloned.1.call-start = ((), (), s32[]{:S(2)}) async-start(), calls=%async_computation.2 | async-start | bytes 1146880 | tf_op jit(solution)/shard_map/reduce_scatter | solution.py:75
  9.5 7.1 %copy-start.3 = (s32[128]{0:T(128)S(1)}, s32[128]{0:T(128)}, u32[]{:S(2)}) copy-start(s32[128]{0:T(128)} %param.12) | copy-start | bytes 1540
  22.8 11.1 %collective-permute-start = (s32[128]{0:T(128)S(1)}, s32[128]{0:T(128)S(1)}, u32[]{:S(2)}, u32[]{:S(2)}) collective-permute-start(s32[128]{0:T(128)S(1)} %get-tuple-element.168), channel_id=1, source_target_pairs={{0,4},{4,8},{8,12},{12,16},{16,20},{20,24},{24,28},{28,32},{32,36}... | collective-permute-start | bytes 1544 | tf_op jit(solution)/shard_map/while/body/eval_jaxpr/ppermute | solution.py:9
  24.8 14.3 %collective-permute-start.1 = (bf16[128,576]{1,0:T(8,128)(2,1)S(1)}, bf16[128,576]{1,0:T(8,128)(2,1)S(1)}, u32[]{:S(2)}, u32[]{:S(2)}) collective-permute-start(bf16[128,576]{1,0:T(8,128)(2,1)S(1)} %get-tuple-element.167), channel_id=1, source_target_pairs={{0,4},{4,8},{8,12},{12,16},{16,20},{20,24},{24,28},{28,32},{32,36}... | collective-permute-start | bytes 442376 | tf_op jit(solution)/shard_map/while/body/eval_jaxpr/ppermute | solution.py:9
  26.1 16.0 %copy-start.1 = (f32[128,16,512]{2,0,1:T(8,128)S(1)}, f32[128,16,512]{2,0,1:T(8,128)}, u32[]{:S(2)}) copy-start(f32[128,16,512]{2,0,1:T(8,128)} %get-tuple-element.166) | copy-start | bytes 12582916 | tf_op jit(solution)/shard_map/while
  43.8 2.0 copy-start.2
  45.8 6.8 %collective-permute-start = (s32[128]{0:T(128)S(1)}, s32[128]{0:T(128)S(1)}, u32[]{:S(2)}, u32[]{:S(2)}) collective-permute-start(s32[128]{0:T(128)S(1)} %get-tuple-element.168), channel_id=1, source_target_pairs={{0,4},{4,8},{8,12},{12,16},{16,20},{20,24},{24,28},{28,32},{32,36}... | collective-permute-start | bytes 1544 | tf_op jit(solution)/shard_map/while/body/eval_jaxpr/ppermute | solution.py:9
  45.8 11.9 %collective-permute-start.1 = (bf16[128,576]{1,0:T(8,128)(2,1)S(1)}, bf16[128,576]{1,0:T(8,128)(2,1)S(1)}, u32[]{:S(2)}, u32[]{:S(2)}) collective-permute-start(bf16[128,576]{1,0:T(8,128)(2,1)S(1)} %get-tuple-element.167), channel_id=1, source_target_pairs={{0,4},{4,8},{8,12},{12,16},{16,20},{20,24},{24,28},{28,32},{32,36}... | collective-permute-start | bytes 442376 | tf_op jit(solution)/shard_map/while/body/eval_jaxpr/ppermute | solution.py:9
  45.8 14.9 %copy-start.1 = (f32[128,16,512]{2,0,1:T(8,128)S(1)}, f32[128,16,512]{2,0,1:T(8,128)}, u32[]{:S(2)}) copy-start(f32[128,16,512]{2,0,1:T(8,128)} %get-tuple-element.166) | copy-start | bytes 12582916 | tf_op jit(solution)/shard_map/while
  62.4 2.0 copy-start.2
  64.3 6.6 %collective-permute-start = (s32[128]{0:T(128)S(1)}, s32[128]{0:T(128)S(1)}, u32[]{:S(2)}, u32[]{:S(2)}) collective-permute-start(s32[128]{0:T(128)S(1)} %get-tuple-element.168), channel_id=1, source_target_pairs={{0,4},{4,8},{8,12},{12,16},{16,20},{20,24},{24,28},{28,32},{32,36}... | collective-permute-start | bytes 1544 | tf_op jit(solution)/shard_map/while/body/eval_jaxpr/ppermute | solution.py:9
  64.3 11.9 %collective-permute-start.1 = (bf16[128,576]{1,0:T(8,128)(2,1)S(1)}, bf16[128,576]{1,0:T(8,128)(2,1)S(1)}, u32[]{:S(2)}, u32[]{:S(2)}) collective-permute-start(bf16[128,576]{1,0:T(8,128)(2,1)S(1)} %get-tuple-element.167), channel_id=1, source_target_pairs={{0,4},{4,8},{8,12},{12,16},{16,20},{20,24},{24,28},{28,32},{32,36}... | collective-permute-start | bytes 442376 | tf_op jit(solution)/shard_map/while/body/eval_jaxpr/ppermute | solution.py:9
  64.3 14.9 %copy-start.1 = (f32[128,16,512]{2,0,1:T(8,128)S(1)}, f32[128,16,512]{2,0,1:T(8,128)}, u32[]{:S(2)}) copy-start(f32[128,16,512]{2,0,1:T(8,128)} %get-tuple-element.166) | copy-start | bytes 12582916 | tf_op jit(solution)/shard_map/while
  80.9 2.0 copy-start.2
  82.9 6.6 %collective-permute-start = (s32[128]{0:T(128)S(1)}, s32[128]{0:T(128)S(1)}, u32[]{:S(2)}, u32[]{:S(2)}) collective-permute-start(s32[128]{0:T(128)S(1)} %get-tuple-element.168), channel_id=1, source_target_pairs={{0,4},{4,8},{8,12},{12,16},{16,20},{20,24},{24,28},{28,32},{32,36}... | collective-permute-start | bytes 1544 | tf_op jit(solution)/shard_map/while/body/eval_jaxpr/ppermute | solution.py:9
  84.5 10.8 %collective-permute-start.1 = (bf16[128,576]{1,0:T(8,128)(2,1)S(1)}, bf16[128,576]{1,0:T(8,128)(2,1)S(1)}, u32[]{:S(2)}, u32[]{:S(2)}) collective-permute-start(bf16[128,576]{1,0:T(8,128)(2,1)S(1)} %get-tuple-element.167), channel_id=1, source_target_pairs={{0,4},{4,8},{8,12},{12,16},{16,20},{20,24},{24,28},{28,32},{32,36}... | collective-permute-start | bytes 442376 | tf_op jit(solution)/shard_map/while/body/eval_jaxpr/ppermute | solution.py:9
  84.5 13.8 %copy-start.1 = (f32[128,16,512]{2,0,1:T(8,128)S(1)}, f32[128,16,512]{2,0,1:T(8,128)}, u32[]{:S(2)}) copy-start(f32[128,16,512]{2,0,1:T(8,128)} %get-tuple-element.166) | copy-start | bytes 12582916 | tf_op jit(solution)/shard_map/while
  100.0 2.0 copy-start.2
  102.0 6.6 %collective-permute-start = (s32[128]{0:T(128)S(1)}, s32[128]{0:T(128)S(1)}, u32[]{:S(2)}, u32[]{:S(2)}) collective-permute-start(s32[128]{0:T(128)S(1)} %get-tuple-element.168), channel_id=1, source_target_pairs={{0,4},{4,8},{8,12},{12,16},{16,20},{20,24},{24,28},{28,32},{32,36}... | collective-permute-start | bytes 1544 | tf_op jit(solution)/shard_map/while/body/eval_jaxpr/ppermute | solution.py:9
  105.4 11.1 %collective-permute-start.1 = (bf16[128,576]{1,0:T(8,128)(2,1)S(1)}, bf16[128,576]{1,0:T(8,128)(2,1)S(1)}, u32[]{:S(2)}, u32[]{:S(2)}) collective-permute-start(bf16[128,576]{1,0:T(8,128)(2,1)S(1)} %get-tuple-element.167), channel_id=1, source_target_pairs={{0,4},{4,8},{8,12},{12,16},{16,20},{20,24},{24,28},{28,32},{32,36}... | collective-permute-start | bytes 442376 | tf_op jit(solution)/shard_map/while/body/eval_jaxpr/ppermute | solution.py:9
  105.4 14.1 %copy-start.1 = (f32[128,16,512]{2,0,1:T(8,128)S(1)}, f32[128,16,512]{2,0,1:T(8,128)}, u32[]{:S(2)}) copy-start(f32[128,16,512]{2,0,1:T(8,128)} %get-tuple-element.166) | copy-start | bytes 12582916 | tf_op jit(solution)/shard_map/while
  121.1 2.0 copy-start.2
  123.1 6.6 %collective-permute-start = (s32[128]{0:T(128)S(1)}, s32[128]{0:T(128)S(1)}, u32[]{:S(2)}, u32[]{:S(2)}) collective-permute-start(s32[128]{0:T(128)S(1)} %get-tuple-element.168), channel_id=1, source_target_pairs={{0,4},{4,8},{8,12},{12,16},{16,20},{20,24},{24,28},{28,32},{32,36}... | collective-permute-start | bytes 1544 | tf_op jit(solution)/shard_map/while/body/eval_jaxpr/ppermute | solution.py:9
  126.1 11.3 %collective-permute-start.1 = (bf16[128,576]{1,0:T(8,128)(2,1)S(1)}, bf16[128,576]{1,0:T(8,128)(2,1)S(1)}, u32[]{:S(2)}, u32[]{:S(2)}) collective-permute-start(bf16[128,576]{1,0:T(8,128)(2,1)S(1)} %get-tuple-element.167), channel_id=1, source_target_pairs={{0,4},{4,8},{8,12},{12,16},{16,20},{20,24},{24,28},{28,32},{32,36}... | collective-permute-start | bytes 442376 | tf_op jit(solution)/shard_map/while/body/eval_jaxpr/ppermute | solution.py:9
  126.1 14.2 %copy-start.1 = (f32[128,16,512]{2,0,1:T(8,128)S(1)}, f32[128,16,512]{2,0,1:T(8,128)}, u32[]{:S(2)}) copy-start(f32[128,16,512]{2,0,1:T(8,128)} %get-tuple-element.166) | copy-start | bytes 12582916 | tf_op jit(solution)/shard_map/while
  142.0 2.0 copy-start.2
  144.0 7.0 %collective-permute-start = (s32[128]{0:T(128)S(1)}, s32[128]{0:T(128)S(1)}, u32[]{:S(2)}, u32[]{:S(2)}) collective-permute-start(s32[128]{0:T(128)S(1)} %get-tuple-element.168), channel_id=1, source_target_pairs={{0,4},{4,8},{8,12},{12,16},{16,20},{20,24},{24,28},{28,32},{32,36}... | collective-permute-start | bytes 1544 | tf_op jit(solution)/shard_map/while/body/eval_jaxpr/ppermute | solution.py:9
  146.3 10.8 %collective-permute-start.1 = (bf16[128,576]{1,0:T(8,128)(2,1)S(1)}, bf16[128,576]{1,0:T(8,128)(2,1)S(1)}, u32[]{:S(2)}, u32[]{:S(2)}) collective-permute-start(bf16[128,576]{1,0:T(8,128)(2,1)S(1)} %get-tuple-element.167), channel_id=1, source_target_pairs={{0,4},{4,8},{8,12},{12,16},{16,20},{20,24},{24,28},{28,32},{32,36}... | collective-permute-start | bytes 442376 | tf_op jit(solution)/shard_map/while/body/eval_jaxpr/ppermute | solution.py:9
  146.3 13.8 %copy-start.1 = (f32[128,16,512]{2,0,1:T(8,128)S(1)}, f32[128,16,512]{2,0,1:T(8,128)}, u32[]{:S(2)}) copy-start(f32[128,16,512]{2,0,1:T(8,128)} %get-tuple-element.166) | copy-start | bytes 12582916 | tf_op jit(solution)/shard_map/while
  161.8 2.0 copy-start.2
  163.7 7.0 %collective-permute-start = (s32[128]{0:T(128)S(1)}, s32[128]{0:T(128)S(1)}, u32[]{:S(2)}, u32[]{:S(2)}) collective-permute-start(s32[128]{0:T(128)S(1)} %get-tuple-element.168), channel_id=1, source_target_pairs={{0,4},{4,8},{8,12},{12,16},{16,20},{20,24},{24,28},{28,32},{32,36}... | collective-permute-start | bytes 1544 | tf_op jit(solution)/shard_map/while/body/eval_jaxpr/ppermute | solution.py:9
  166.5 10.7 %collective-permute-start.1 = (bf16[128,576]{1,0:T(8,128)(2,1)S(1)}, bf16[128,576]{1,0:T(8,128)(2,1)S(1)}, u32[]{:S(2)}, u32[]{:S(2)}) collective-permute-start(bf16[128,576]{1,0:T(8,128)(2,1)S(1)} %get-tuple-element.167), channel_id=1, source_target_pairs={{0,4},{4,8},{8,12},{12,16},{16,20},{20,24},{24,28},{28,32},{32,36}... | collective-permute-start | bytes 442376 | tf_op jit(solution)/shard_map/while/body/eval_jaxpr/ppermute | solution.py:9
  166.5 13.6 %copy-start.1 = (f32[128,16,512]{2,0,1:T(8,128)S(1)}, f32[128,16,512]{2,0,1:T(8,128)}, u32[]{:S(2)}) copy-start(f32[128,16,512]{2,0,1:T(8,128)} %get-tuple-element.166) | copy-start | bytes 12582916 | tf_op jit(solution)/shard_map/while
  181.9 2.0 copy-start.2
  183.8 6.6 %collective-permute-start = (s32[128]{0:T(128)S(1)}, s32[128]{0:T(128)S(1)}, u32[]{:S(2)}, u32[]{:S(2)}) collective-permute-start(s32[128]{0:T(128)S(1)} %get-tuple-element.168), channel_id=1, source_target_pairs={{0,4},{4,8},{8,12},{12,16},{16,20},{20,24},{24,28},{28,32},{32,36}... | collective-permute-start | bytes 1544 | tf_op jit(solution)/shard_map/while/body/eval_jaxpr/ppermute | solution.py:9
  187.0 11.2 %collective-permute-start.1 = (bf16[128,576]{1,0:T(8,128)(2,1)S(1)}, bf16[128,576]{1,0:T(8,128)(2,1)S(1)}, u32[]{:S(2)}, u32[]{:S(2)}) collective-permute-start(bf16[128,576]{1,0:T(8,128)(2,1)S(1)} %get-tuple-element.167), channel_id=1, source_target_pairs={{0,4},{4,8},{8,12},{12,16},{16,20},{20,24},{24,28},{28,32},{32,36}... | collective-permute-start | bytes 442376 | tf_op jit(solution)/shard_map/while/body/eval_jaxpr/ppermute | solution.py:9
  187.0 14.1 %copy-start.1 = (f32[128,16,512]{2,0,1:T(8,128)S(1)}, f32[128,16,512]{2,0,1:T(8,128)}, u32[]{:S(2)}) copy-start(f32[128,16,512]{2,0,1:T(8,128)} %get-tuple-element.166) | copy-start | bytes 12582916 | tf_op jit(solution)/shard_map/while
  202.8 2.0 copy-start.2
  204.8 6.6 %collective-permute-start = (s32[128]{0:T(128)S(1)}, s32[128]{0:T(128)S(1)}, u32[]{:S(2)}, u32[]{:S(2)}) collective-permute-start(s32[128]{0:T(128)S(1)} %get-tuple-element.168), channel_id=1, source_target_pairs={{0,4},{4,8},{8,12},{12,16},{16,20},{20,24},{24,28},{28,32},{32,36}... | collective-permute-start | bytes 1544 | tf_op jit(solution)/shard_map/while/body/eval_jaxpr/ppermute | solution.py:9
  207.1 10.2 %collective-permute-start.1 = (bf16[128,576]{1,0:T(8,128)(2,1)S(1)}, bf16[128,576]{1,0:T(8,128)(2,1)S(1)}, u32[]{:S(2)}, u32[]{:S(2)}) collective-permute-start(bf16[128,576]{1,0:T(8,128)(2,1)S(1)} %get-tuple-element.167), channel_id=1, source_target_pairs={{0,4},{4,8},{8,12},{12,16},{16,20},{20,24},{24,28},{28,32},{32,36}... | collective-permute-start | bytes 442376 | tf_op jit(solution)/shard_map/while/body/eval_jaxpr/ppermute | solution.py:9
  207.1 13.1 %copy-start.1 = (f32[128,16,512]{2,0,1:T(8,128)S(1)}, f32[128,16,512]{2,0,1:T(8,128)}, u32[]{:S(2)}) copy-start(f32[128,16,512]{2,0,1:T(8,128)} %get-tuple-element.166) | copy-start | bytes 12582916 | tf_op jit(solution)/shard_map/while
  221.9 2.0 copy-start.2
  223.9 6.6 %collective-permute-start = (s32[128]{0:T(128)S(1)}, s32[128]{0:T(128)S(1)}, u32[]{:S(2)}, u32[]{:S(2)}) collective-permute-start(s32[128]{0:T(128)S(1)} %get-tuple-element.168), channel_id=1, source_target_pairs={{0,4},{4,8},{8,12},{12,16},{16,20},{20,24},{24,28},{28,32},{32,36}... | collective-permute-start | bytes 1544 | tf_op jit(solution)/shard_map/while/body/eval_jaxpr/ppermute | solution.py:9
  227.0 11.1 %collective-permute-start.1 = (bf16[128,576]{1,0:T(8,128)(2,1)S(1)}, bf16[128,576]{1,0:T(8,128)(2,1)S(1)}, u32[]{:S(2)}, u32[]{:S(2)}) collective-permute-start(bf16[128,576]{1,0:T(8,128)(2,1)S(1)} %get-tuple-element.167), channel_id=1, source_target_pairs={{0,4},{4,8},{8,12},{12,16},{16,20},{20,24},{24,28},{28,32},{32,36}... | collective-permute-start | bytes 442376 | tf_op jit(solution)/shard_map/while/body/eval_jaxpr/ppermute | solution.py:9
  227.1 14.0 %copy-start.1 = (f32[128,16,512]{2,0,1:T(8,128)S(1)}, f32[128,16,512]{2,0,1:T(8,128)}, u32[]{:S(2)}) copy-start(f32[128,16,512]{2,0,1:T(8,128)} %get-tuple-element.166) | copy-start | bytes 12582916 | tf_op jit(solution)/shard_map/while
  242.8 2.0 copy-start.2
  244.8 6.6 %collective-permute-start = (s32[128]{0:T(128)S(1)}, s32[128]{0:T(128)S(1)}, u32[]{:S(2)}, u32[]{:S(2)}) collective-permute-start(s32[128]{0:T(128)S(1)} %get-tuple-element.168), channel_id=1, source_target_pairs={{0,4},{4,8},{8,12},{12,16},{16,20},{20,24},{24,28},{28,32},{32,36}... | collective-permute-start | bytes 1544 | tf_op jit(solution)/shard_map/while/body/eval_jaxpr/ppermute | solution.py:9
  247.7 11.2 %collective-permute-start.1 = (bf16[128,576]{1,0:T(8,128)(2,1)S(1)}, bf16[128,576]{1,0:T(8,128)(2,1)S(1)}, u32[]{:S(2)}, u32[]{:S(2)}) collective-permute-start(bf16[128,576]{1,0:T(8,128)(2,1)S(1)} %get-tuple-element.167), channel_id=1, source_target_pairs={{0,4},{4,8},{8,12},{12,16},{16,20},{20,24},{24,28},{28,32},{32,36}... | collective-permute-start | bytes 442376 | tf_op jit(solution)/shard_map/while/body/eval_jaxpr/ppermute | solution.py:9
  247.7 14.1 %copy-start.1 = (f32[128,16,512]{2,0,1:T(8,128)S(1)}, f32[128,16,512]{2,0,1:T(8,128)}, u32[]{:S(2)}) copy-start(f32[128,16,512]{2,0,1:T(8,128)} %get-tuple-element.166) | copy-start | bytes 12582916 | tf_op jit(solution)/shard_map/while
  263.5 2.0 copy-start.2
  265.5 6.6 %collective-permute-start = (s32[128]{0:T(128)S(1)}, s32[128]{0:T(128)S(1)}, u32[]{:S(2)}, u32[]{:S(2)}) collective-permute-start(s32[128]{0:T(128)S(1)} %get-tuple-element.168), channel_id=1, source_target_pairs={{0,4},{4,8},{8,12},{12,16},{16,20},{20,24},{24,28},{28,32},{32,36}... | collective-permute-start | bytes 1544 | tf_op jit(solution)/shard_map/while/body/eval_jaxpr/ppermute | solution.py:9
  267.8 10.5 %collective-permute-start.1 = (bf16[128,576]{1,0:T(8,128)(2,1)S(1)}, bf16[128,576]{1,0:T(8,128)(2,1)S(1)}, u32[]{:S(2)}, u32[]{:S(2)}) collective-permute-start(bf16[128,576]{1,0:T(8,128)(2,1)S(1)} %get-tuple-element.167), channel_id=1, source_target_pairs={{0,4},{4,8},{8,12},{12,16},{16,20},{20,24},{24,28},{28,32},{32,36}... | collective-permute-start | bytes 442376 | tf_op jit(solution)/shard_map/while/body/eval_jaxpr/ppermute | solution.py:9
  267.8 13.4 %copy-start.1 = (f32[128,16,512]{2,0,1:T(8,128)S(1)}, f32[128,16,512]{2,0,1:T(8,128)}, u32[]{:S(2)}) copy-start(f32[128,16,512]{2,0,1:T(8,128)} %get-tuple-element.166) | copy-start | bytes 12582916 | tf_op jit(solution)/shard_map/while
  282.9 2.0 copy-start.2
  284.9 6.6 %collective-permute-start = (s32[128]{0:T(128)S(1)}, s32[128]{0:T(128)S(1)}, u32[]{:S(2)}, u32[]{:S(2)}) collective-permute-start(s32[128]{0:T(128)S(1)} %get-tuple-element.168), channel_id=1, source_target_pairs={{0,4},{4,8},{8,12},{12,16},{16,20},{20,24},{24,28},{28,32},{32,36}... | collective-permute-start | bytes 1544 | tf_op jit(solution)/shard_map/while/body/eval_jaxpr/ppermute | solution.py:9
  288.1 11.2 %collective-permute-start.1 = (bf16[128,576]{1,0:T(8,128)(2,1)S(1)}, bf16[128,576]{1,0:T(8,128)(2,1)S(1)}, u32[]{:S(2)}, u32[]{:S(2)}) collective-permute-start(bf16[128,576]{1,0:T(8,128)(2,1)S(1)} %get-tuple-element.167), channel_id=1, source_target_pairs={{0,4},{4,8},{8,12},{12,16},{16,20},{20,24},{24,28},{28,32},{32,36}... | collective-permute-start | bytes 442376 | tf_op jit(solution)/shard_map/while/body/eval_jaxpr/ppermute | solution.py:9
  288.1 14.1 %copy-start.1 = (f32[128,16,512]{2,0,1:T(8,128)S(1)}, f32[128,16,512]{2,0,1:T(8,128)}, u32[]{:S(2)}) copy-start(f32[128,16,512]{2,0,1:T(8,128)} %get-tuple-element.166) | copy-start | bytes 12582916 | tf_op jit(solution)/shard_map/while
  303.9 2.0 copy-start.2
  305.9 6.6 %collective-permute-start = (s32[128]{0:T(128)S(1)}, s32[128]{0:T(128)S(1)}, u32[]{:S(2)}, u32[]{:S(2)}) collective-permute-start(s32[128]{0:T(128)S(1)} %get-tuple-element.168), channel_id=1, source_target_pairs={{0,4},{4,8},{8,12},{12,16},{16,20},{20,24},{24,28},{28,32},{32,36}... | collective-permute-start | bytes 1544 | tf_op jit(solution)/shard_map/while/body/eval_jaxpr/ppermute | solution.py:9
  308.2 10.0 %collective-permute-start.1 = (bf16[128,576]{1,0:T(8,128)(2,1)S(1)}, bf16[128,576]{1,0:T(8,128)(2,1)S(1)}, u32[]{:S(2)}, u32[]{:S(2)}) collective-permute-start(bf16[128,576]{1,0:T(8,128)(2,1)S(1)} %get-tuple-element.167), channel_id=1, source_target_pairs={{0,4},{4,8},{8,12},{12,16},{16,20},{20,24},{24,28},{28,32},{32,36}... | collective-permute-start | bytes 442376 | tf_op jit(solution)/shard_map/while/body/eval_jaxpr/ppermute | solution.py:9
  308.2 13.0 %copy-start.1 = (f32[128,16,512]{2,0,1:T(8,128)S(1)}, f32[128,16,512]{2,0,1:T(8,128)}, u32[]{:S(2)}) copy-start(f32[128,16,512]{2,0,1:T(8,128)} %get-tuple-element.166) | copy-start | bytes 12582916 | tf_op jit(solution)/shard_map/while
  322.9 2.0 copy-start.2
Sparse Core Ops, SparseCore 0:
  9.1 384.5 all-gather.1
  404.9 36.5 reduce-scatter.1
where the time goes:
time: 449 us; the launch traced here: 448 us
  waiting for transfers between devices  267 us (59%)
  matrix products  89.5 us (20%)
  starting transfers between devices  36.2 us (8%)
  local copies, waits for them, and re-layouts  35.8 us (8%)
  between operations  13.5 us (3%)
  other arithmetic  4.66 us (1%)
    ppermute x30, waiting for transfers between devices, from_behind(): return lax.ppermute(x, axis, [(i, (i + by) % count) for i in range(count)])  165 us
    all_gather x1, waiting for transfers between devices, local(): lax.all_gather(w_o, 'ctx', axis=1, tiled=True)  64.8 us
    dot_general x16, matrix products, absorb(): jnp.einsum('thl,kl->thk', q_latent, keys[:, :lat_dim], preferred_element_...  38.4 us
    reduce_scatter x1, waiting for transfers between devices, local(): lax.psum_scatter(partial_out.astype(jnp.float32).astype(jnp.bfloat16), 'h...  36.7 us
    ppermute x30, starting transfers between devices, from_behind(): return lax.ppermute(x, axis, [(i, (i + by) % count) for i in range(count)])  36.2 us
    while x105, local copies, waits for them, and re-layouts  29.7 us
    dot_general x16, matrix products, absorb(): jnp.einsum('thk,kl->thl', weights.astype(jnp.bfloat16), keys[:, :lat_dim]...  27.8 us
    dot_general x1, matrix products, local(): lax.dot_general(lax.all_gather(w_o, 'ctx', axis=1, tiled=True), head_out,...  11.1 us
  transfers between devices with their start and end apart: 32, of which 32 were waited for; matrix products, arithmetic and copies ran while one was open for 20% of the time, Pallas kernels for 0%

commit v1 on v0

--- a/solution.py
+++ b/solution.py
@@ -65,7 +65,9 @@
     ).astype(jnp.bfloat16)
     head_out = head_out.reshape(tok_rows, heads * w_uv.shape[2])
     product = lax.dot_general(
-        lax.all_gather(w_o, "ctx", axis=1, tiled=True),
+        jnp.concatenate(
+            lax.all_to_all(jnp.stack([w_o] * lax.axis_size("ctx")), "ctx", 0, 0), axis=1
+        ),
         head_out,
         (((0,), (1,)), ((), ())),
         preferred_element_type=jnp.float32,

time: 449 us -> 644 us (1.43)
  waiting for transfers between devices: 267 us -> 478 us
  starting transfers between devices: 36.2 us -> 16.2 us
    ppermute x30, waiting for transfers between devices: 165 us -> 420 us  [from_behind(): return lax.ppermute(x, axis, [(i, (i + by) % count) for i in range(count)])]
    all_gather x1 -> x0, waiting for transfers between devices: 64.8 us -> none  [local(): lax.all_gather(w_o, 'ctx', axis=1, tiled=True)]
    ppermute x30, starting transfers between devices: 36.2 us -> 2.2 us  [from_behind(): return lax.ppermute(x, axis, [(i, (i + by) % count) for i in range(count)])]
    reduce_scatter x1, waiting for transfers between devices: 36.7 us -> 57.5 us  [local(): lax.psum_scatter(partial_out.astype(jnp.float32).astype(jnp.bfloat16), 'h...]
    all_to_all x0 -> x1, starting transfers between devices: none -> 13.9 us  [local(): lax.all_to_all(jnp.stack([w_o] * lax.axis_size('ctx')), 'ctx', 0, 0)]
    another operation x0 -> x1, local copies, waits for them, and re-layouts: none -> 8.13 us  [local(): jnp.stack([w_o] * lax.axis_size('ctx'))]
  transfers between devices with their start and end apart: 32 -> 32, of which waited for: 32 -> 31; matrix products, arithmetic and copies ran while one was open for 20% -> 13% of each run, Pallas kernels for 0% -> 0%
where the time goes in v1:
time: 644 us; the launch traced here: 643 us
  waiting for transfers between devices  478 us (74%)
  matrix products  87.7 us (14%)
  local copies, waits for them, and re-layouts  41.7 us (6%)
  starting transfers between devices  16.2 us (3%)
  between operations  13.5 us (2%)
    ppermute x30, waiting for transfers between devices, from_behind(): return lax.ppermute(x, axis, [(i, (i + by) % count) for i in range(count)])  420 us
    reduce_scatter x1, waiting for transfers between devices, local(): lax.psum_scatter(partial_out.astype(jnp.float32).astype(jnp.bfloat16), 'h...  57.5 us
    dot_general x16, matrix products, absorb(): jnp.einsum('thl,kl->thk', q_latent, keys[:, :lat_dim], preferred_element_...  38.3 us
    while x105, local copies, waits for them, and re-layouts  29.3 us
    dot_general x16, matrix products, absorb(): jnp.einsum('thk,kl->thl', weights.astype(jnp.bfloat16), keys[:, :lat_dim]...  27.8 us
    all_to_all x1, starting transfers between devices, local(): lax.all_to_all(jnp.stack([w_o] * lax.axis_size('ctx')), 'ctx', 0, 0)  13.9 us
  transfers between devices with their start and end apart: 32, of which 31 were waited for; matrix products, arithmetic and copies ran while one was open for 13% of the time, Pallas kernels for 0%

profile of v1, /device:TPU:1, one launch (start us, length us, event | category | flops | bytes accessed | tf_op | source)
XLA Modules:
  0.0 643.1 jit_solution(9916036308610209253)
XLA Ops:
  6.5 8.1 %stack.2 = bf16[64,2048,56]{1,2,0:T(8,128)(2,1)} broadcast(bf16[2048,56]{0,1:T(8,128)(2,1)} %param.15), dimensions={1,2} | broadcast | bytes 14909440 | tf_op jit(solution)/shard_map/stack | solution.py:69
  14.7 13.9 %all-to-all-start = ((bf16[64,2048,56]{1,2,0:T(8,128)(2,1)}), bf16[64,2048,56]{1,2,0:T(8,128)(2,1)}, u32[]{:S(2)}, u32[]{:S(2)}) async-start(bf16[64,2048,56]{1,2,0:T(8,128)(2,1)} %stack.2), calls=%async_computation | async-start | bytes 29360128 | tf_op jit(solution)/shard_map/all_to_all | solution.py:69
  29.1 2.1 convert_bitcast_fusion
  31.2 3.9 copy.29
  35.5 2.1 fusion.22
  37.9 2.7 convolution_add_fusion.1
  40.6 523.1 %while.18 = (s32[]{:T(128)}, f32[128,16]{0,1:T(8,128)S(1)}, f32[128,16]{0,1:T(8,128)S(1)}, f32[128,16,512]{2,0,1:T(8,128)}, bf16[128,576]{1,0:T(8,128)(2,1)S(1)}...) while((s32[]{:T(128)}, f32[128,16]{0,1:T(8,128)S(1)}, ...), condition=%wide.region_5.6_spmd, body=%wide.region_2.5_spmd.sunk | while | flops 575164416 | bytes 50925804 | solution.py:59
  42.7 286.5 %collective-permute-done = s32[128]{0:T(128)S(1)} collective-permute-done((s32[128]{0:T(128)S(1)}, s32[128]{0:T(128)S(1)}, u32[]{:S(2)}, u32[]{:S(2)}) %collective-permute-start) | collective-permute-done | bytes 544 | tf_op jit(solution)/shard_map/while/body/eval_jaxpr/ppermute | solution.py:9
  329.3 10.4 %collective-permute-done.1 = bf16[128,576]{1,0:T(8,128)(2,1)S(1)} collective-permute-done((bf16[128,576]{1,0:T(8,128)(2,1)S(1)}, bf16[128,576]{1,0:T(8,128)(2,1)S(1)}, u32[]{:S(2)}, u32[]{:S(2)}) %collective-permute-start.1) | collective-permute-done | bytes 147488 | tf_op jit(solution)/shard_map/while/body/eval_jaxpr/ppermute | solution.py:9
  340.0 2.4 select_reduce_fusion.2
  344.4 1.9 copy-done.2
  346.4 6.6 %collective-permute-done = s32[128]{0:T(128)S(1)} collective-permute-done((s32[128]{0:T(128)S(1)}, s32[128]{0:T(128)S(1)}, u32[]{:S(2)}, u32[]{:S(2)}) %collective-permute-start) | collective-permute-done | bytes 544 | tf_op jit(solution)/shard_map/while/body/eval_jaxpr/ppermute | solution.py:9
  353.1 5.5 collective-permute-done.1
  358.9 2.4 select_reduce_fusion.2
  363.2 1.9 copy-done.2
  365.2 6.6 %collective-permute-done = s32[128]{0:T(128)S(1)} collective-permute-done((s32[128]{0:T(128)S(1)}, s32[128]{0:T(128)S(1)}, u32[]{:S(2)}, u32[]{:S(2)}) %collective-permute-start) | collective-permute-done | bytes 544 | tf_op jit(solution)/shard_map/while/body/eval_jaxpr/ppermute | solution.py:9
  371.9 1.7 collective-permute-done.1
  373.9 2.4 select_reduce_fusion.2
  378.2 1.9 copy-done.2
  380.2 6.6 %collective-permute-done = s32[128]{0:T(128)S(1)} collective-permute-done((s32[128]{0:T(128)S(1)}, s32[128]{0:T(128)S(1)}, u32[]{:S(2)}, u32[]{:S(2)}) %collective-permute-start) | collective-permute-done | bytes 544 | tf_op jit(solution)/shard_map/while/body/eval_jaxpr/ppermute | solution.py:9
  386.9 1.7 collective-permute-done.1
  388.9 2.4 select_reduce_fusion.2
  393.2 1.9 copy-done.2
  395.2 6.6 %collective-permute-done = s32[128]{0:T(128)S(1)} collective-permute-done((s32[128]{0:T(128)S(1)}, s32[128]{0:T(128)S(1)}, u32[]{:S(2)}, u32[]{:S(2)}) %collective-permute-start) | collective-permute-done | bytes 544 | tf_op jit(solution)/shard_map/while/body/eval_jaxpr/ppermute | solution.py:9
  401.9 1.7 collective-permute-done.1
  403.9 2.4 select_reduce_fusion.2
  408.3 1.9 copy-done.2
  410.2 6.6 %collective-permute-done = s32[128]{0:T(128)S(1)} collective-permute-done((s32[128]{0:T(128)S(1)}, s32[128]{0:T(128)S(1)}, u32[]{:S(2)}, u32[]{:S(2)}) %collective-permute-start) | collective-permute-done | bytes 544 | tf_op jit(solution)/shard_map/while/body/eval_jaxpr/ppermute | solution.py:9
  418.9 2.4 select_reduce_fusion.2
  423.3 1.9 copy-done.2
  425.2 6.6 %collective-permute-done = s32[128]{0:T(128)S(1)} collective-permute-done((s32[128]{0:T(128)S(1)}, s32[128]{0:T(128)S(1)}, u32[]{:S(2)}, u32[]{:S(2)}) %collective-permute-start) | collective-permute-done | bytes 544 | tf_op jit(solution)/shard_map/while/body/eval_jaxpr/ppermute | solution.py:9
  433.9 2.4 select_reduce_fusion.2
  438.3 1.9 copy-done.2
  440.2 6.6 %collective-permute-done = s32[128]{0:T(128)S(1)} collective-permute-done((s32[128]{0:T(128)S(1)}, s32[128]{0:T(128)S(1)}, u32[]{:S(2)}, u32[]{:S(2)}) %collective-permute-start) | collective-permute-done | bytes 544 | tf_op jit(solution)/shard_map/while/body/eval_jaxpr/ppermute | solution.py:9
  446.9 1.7 collective-permute-done.1
  448.9 2.4 select_reduce_fusion.2
  453.3 1.9 copy-done.2
  455.2 6.6 %collective-permute-done = s32[128]{0:T(128)S(1)} collective-permute-done((s32[128]{0:T(128)S(1)}, s32[128]{0:T(128)S(1)}, u32[]{:S(2)}, u32[]{:S(2)}) %collective-permute-start) | collective-permute-done | bytes 544 | tf_op jit(solution)/shard_map/while/body/eval_jaxpr/ppermute | solution.py:9
  463.9 2.4 select_reduce_fusion.2
  468.3 1.9 copy-done.2
  470.2 6.6 %collective-permute-done = s32[128]{0:T(128)S(1)} collective-permute-done((s32[128]{0:T(128)S(1)}, s32[128]{0:T(128)S(1)}, u32[]{:S(2)}, u32[]{:S(2)}) %collective-permute-start) | collective-permute-done | bytes 544 | tf_op jit(solution)/shard_map/while/body/eval_jaxpr/ppermute | solution.py:9
  478.9 2.4 select_reduce_fusion.2
  483.3 1.9 copy-done.2
  485.2 6.6 %collective-permute-done = s32[128]{0:T(128)S(1)} collective-permute-done((s32[128]{0:T(128)S(1)}, s32[128]{0:T(128)S(1)}, u32[]{:S(2)}, u32[]{:S(2)}) %collective-permute-start) | collective-permute-done | bytes 544 | tf_op jit(solution)/shard_map/while/body/eval_jaxpr/ppermute | solution.py:9
  493.9 2.4 select_reduce_fusion.2
  498.3 1.9 copy-done.2
  500.2 6.8 %collective-permute-done = s32[128]{0:T(128)S(1)} collective-permute-done((s32[128]{0:T(128)S(1)}, s32[128]{0:T(128)S(1)}, u32[]{:S(2)}, u32[]{:S(2)}) %collective-permute-start) | collective-permute-done | bytes 544 | tf_op jit(solution)/shard_map/while/body/eval_jaxpr/ppermute | solution.py:9
  508.9 2.4 select_reduce_fusion.2
  513.3 1.9 copy-done.2
  515.2 6.9 %collective-permute-done = s32[128]{0:T(128)S(1)} collective-permute-done((s32[128]{0:T(128)S(1)}, s32[128]{0:T(128)S(1)}, u32[]{:S(2)}, u32[]{:S(2)}) %collective-permute-start) | collective-permute-done | bytes 544 | tf_op jit(solution)/shard_map/while/body/eval_jaxpr/ppermute | solution.py:9
  522.3 2.4 collective-permute-done.1
  524.9 2.4 select_reduce_fusion.2
  529.3 1.9 copy-done.2
  531.3 6.6 %collective-permute-done = s32[128]{0:T(128)S(1)} collective-permute-done((s32[128]{0:T(128)S(1)}, s32[128]{0:T(128)S(1)}, u32[]{:S(2)}, u32[]{:S(2)}) %collective-permute-start) | collective-permute-done | bytes 544 | tf_op jit(solution)/shard_map/while/body/eval_jaxpr/ppermute | solution.py:9
  538.0 3.3 collective-permute-done.1
  541.6 2.4 select_reduce_fusion.2
  545.9 1.9 copy-done.2
  547.9 6.6 %collective-permute-done = s32[128]{0:T(128)S(1)} collective-permute-done((s32[128]{0:T(128)S(1)}, s32[128]{0:T(128)S(1)}, u32[]{:S(2)}, u32[]{:S(2)}) %collective-permute-start) | collective-permute-done | bytes 544 | tf_op jit(solution)/shard_map/while/body/eval_jaxpr/ppermute | solution.py:9
  554.6 2.4 collective-permute-done.1
  557.3 2.4 select_reduce_fusion.2
  561.7 1.9 copy-done.2
  563.6 4.0 fusion.12
  567.6 11.1 %convolution_convert_fusion = bf16[128,3584]{1,0:T(8,128)(2,1)} fusion(bf16[128,2048]{0,1:T(8,128)(2,1)S(1)} %bitcast.47, bf16[2048,3584]{0,1:T(8,128)(2,1)} %bitcast.9), kind=kOutput, calls=%fused_computation.17 | convolution fusion | flops 1879506944 | bytes 16121856 | tf_op jit(solution)/shard_map/dot_general | solution.py:67
  578.8 57.5 %reduce-scatter.2.cloned.1.call-done = bf16[32,3584]{1,0:T(8,128)(2,1)} async-done(((bf16[128,3584]{1,0:T(8,128)(2,1)}), bf16[32,3584]{1,0:T(8,128)(2,1)}) %reduce-scatter.2.cloned.1.call-update) | async-done | bytes 229392 | tf_op jit(solution)/shard_map/reduce_scatter | solution.py:77
  (236 shorter events, 47.1 us)
Async XLA Ops:
  6.5 22.5 %copy-start = (bf16[16,128,512]{2,1,0:T(8,128)(2,1)S(1)}, bf16[16,128,512]{2,1,0:T(8,128)(2,1)}, u32[]{:S(2)}) copy-start(bf16[16,128,512]{2,1,0:T(8,128)(2,1)} %param.13) | copy-start | bytes 6291460
  14.7 14.0 %copy-start.6 = (s32[128]{0:T(128)S(1)}, s32[128]{0:T(128)}, u32[]{:S(2)}) copy-start(s32[128]{0:T(128)} %param.12) | copy-start | bytes 1540
  14.7 14.0 %copy-start.5 = (bf16[128,576]{0,1:T(8,128)(2,1)S(1)}, bf16[128,576]{0,1:T(8,128)(2,1)}, u32[]{:S(2)}) copy-start(bf16[128,576]{0,1:T(8,128)(2,1)} %param.11) | copy-start | bytes 442372
  14.7 14.2 %copy-start.4 = (bf16[128,1024]{1,0:T(8,128)(2,1)S(1)}, bf16[128,1024]{1,0:T(8,128)(2,1)}, u32[]{:S(2)}) copy-start(bf16[128,1024]{1,0:T(8,128)(2,1)} %param.10) | copy-start | bytes 786436
  14.7 14.4 %copy-start.3 = (bf16[128,16,128]{2,1,0:T(8,128)(2,1)S(1)}, bf16[128,16,128]{2,1,0:T(8,128)(2,1)}, u32[]{:S(2)}) copy-start(bf16[128,16,128]{2,1,0:T(8,128)(2,1)} %param.9) | copy-start | bytes 1572868
  14.7 552.9 %all-to-all-start = ((bf16[64,2048,56]{1,2,0:T(8,128)(2,1)}), bf16[64,2048,56]{1,2,0:T(8,128)(2,1)}, u32[]{:S(2)}, u32[]{:S(2)}) async-start(bf16[64,2048,56]{1,2,0:T(8,128)(2,1)} %stack.2), calls=%async_computation | async-start | bytes 29360128 | tf_op jit(solution)/shard_map/all_to_all | solution.py:69
  28.6 607.6 %reduce-scatter.2.cloned.1.call-start = ((), (), s32[]{:S(2)}) async-start(), calls=%async_computation.2 | async-start | bytes 1146880 | tf_op jit(solution)/shard_map/reduce_scatter | solution.py:77
  40.6 288.7 %collective-permute-start = (s32[128]{0:T(128)S(1)}, s32[128]{0:T(128)S(1)}, u32[]{:S(2)}, u32[]{:S(2)}) collective-permute-start(s32[128]{0:T(128)S(1)} %get-tuple-element.177), channel_id=1, source_target_pairs={{0,4},{4,8},{8,12},{12,16},{16,20},{20,24},{24,28},{28,32},{32,36}... | collective-permute-start | bytes 1544 | tf_op jit(solution)/shard_map/while/body/eval_jaxpr/ppermute | solution.py:9
  41.5 298.2 %collective-permute-start.1 = (bf16[128,576]{1,0:T(8,128)(2,1)S(1)}, bf16[128,576]{1,0:T(8,128)(2,1)S(1)}, u32[]{:S(2)}, u32[]{:S(2)}) collective-permute-start(bf16[128,576]{1,0:T(8,128)(2,1)S(1)} %get-tuple-element.176), channel_id=1, source_target_pairs={{0,4},{4,8},{8,12},{12,16},{16,20},{20,24},{24,28},{28,32},{32,36}... | collective-permute-start | bytes 442376 | tf_op jit(solution)/shard_map/while/body/eval_jaxpr/ppermute | solution.py:9
  42.7 300.0 %copy-start.1 = (f32[128,16,512]{2,0,1:T(8,128)S(1)}, f32[128,16,512]{2,0,1:T(8,128)}, u32[]{:S(2)}) copy-start(f32[128,16,512]{2,0,1:T(8,128)} %get-tuple-element.175) | copy-start | bytes 12582916 | tf_op jit(solution)/shard_map/while
  344.4 1.9 copy-start.2
  346.3 6.6 %collective-permute-start = (s32[128]{0:T(128)S(1)}, s32[128]{0:T(128)S(1)}, u32[]{:S(2)}, u32[]{:S(2)}) collective-permute-start(s32[128]{0:T(128)S(1)} %get-tuple-element.177), channel_id=1, source_target_pairs={{0,4},{4,8},{8,12},{12,16},{16,20},{20,24},{24,28},{28,32},{32,36}... | collective-permute-start | bytes 1544 | tf_op jit(solution)/shard_map/while/body/eval_jaxpr/ppermute | solution.py:9
  346.3 12.2 %collective-permute-start.1 = (bf16[128,576]{1,0:T(8,128)(2,1)S(1)}, bf16[128,576]{1,0:T(8,128)(2,1)S(1)}, u32[]{:S(2)}, u32[]{:S(2)}) collective-permute-start(bf16[128,576]{1,0:T(8,128)(2,1)S(1)} %get-tuple-element.176), channel_id=1, source_target_pairs={{0,4},{4,8},{8,12},{12,16},{16,20},{20,24},{24,28},{28,32},{32,36}... | collective-permute-start | bytes 442376 | tf_op jit(solution)/shard_map/while/body/eval_jaxpr/ppermute | solution.py:9
  346.4 15.2 %copy-start.1 = (f32[128,16,512]{2,0,1:T(8,128)S(1)}, f32[128,16,512]{2,0,1:T(8,128)}, u32[]{:S(2)}) copy-start(f32[128,16,512]{2,0,1:T(8,128)} %get-tuple-element.175) | copy-start | bytes 12582916 | tf_op jit(solution)/shard_map/while
  363.2 1.9 copy-start.2
  365.2 6.6 %collective-permute-start = (s32[128]{0:T(128)S(1)}, s32[128]{0:T(128)S(1)}, u32[]{:S(2)}, u32[]{:S(2)}) collective-permute-start(s32[128]{0:T(128)S(1)} %get-tuple-element.177), channel_id=1, source_target_pairs={{0,4},{4,8},{8,12},{12,16},{16,20},{20,24},{24,28},{28,32},{32,36}... | collective-permute-start | bytes 1544 | tf_op jit(solution)/shard_map/while/body/eval_jaxpr/ppermute | solution.py:9
  365.2 8.4 %collective-permute-start.1 = (bf16[128,576]{1,0:T(8,128)(2,1)S(1)}, bf16[128,576]{1,0:T(8,128)(2,1)S(1)}, u32[]{:S(2)}, u32[]{:S(2)}) collective-permute-start(bf16[128,576]{1,0:T(8,128)(2,1)S(1)} %get-tuple-element.176), channel_id=1, source_target_pairs={{0,4},{4,8},{8,12},{12,16},{16,20},{20,24},{24,28},{28,32},{32,36}... | collective-permute-start | bytes 442376 | tf_op jit(solution)/shard_map/while/body/eval_jaxpr/ppermute | solution.py:9
  365.2 11.4 %copy-start.1 = (f32[128,16,512]{2,0,1:T(8,128)S(1)}, f32[128,16,512]{2,0,1:T(8,128)}, u32[]{:S(2)}) copy-start(f32[128,16,512]{2,0,1:T(8,128)} %get-tuple-element.175) | copy-start | bytes 12582916 | tf_op jit(solution)/shard_map/while
  378.2 1.9 copy-start.2
  380.2 6.6 %collective-permute-start = (s32[128]{0:T(128)S(1)}, s32[128]{0:T(128)S(1)}, u32[]{:S(2)}, u32[]{:S(2)}) collective-permute-start(s32[128]{0:T(128)S(1)} %get-tuple-element.177), channel_id=1, source_target_pairs={{0,4},{4,8},{8,12},{12,16},{16,20},{20,24},{24,28},{28,32},{32,36}... | collective-permute-start | bytes 1544 | tf_op jit(solution)/shard_map/while/body/eval_jaxpr/ppermute | solution.py:9
  380.2 8.4 %collective-permute-start.1 = (bf16[128,576]{1,0:T(8,128)(2,1)S(1)}, bf16[128,576]{1,0:T(8,128)(2,1)S(1)}, u32[]{:S(2)}, u32[]{:S(2)}) collective-permute-start(bf16[128,576]{1,0:T(8,128)(2,1)S(1)} %get-tuple-element.176), channel_id=1, source_target_pairs={{0,4},{4,8},{8,12},{12,16},{16,20},{20,24},{24,28},{28,32},{32,36}... | collective-permute-start | bytes 442376 | tf_op jit(solution)/shard_map/while/body/eval_jaxpr/ppermute | solution.py:9
  380.2 11.4 %copy-start.1 = (f32[128,16,512]{2,0,1:T(8,128)S(1)}, f32[128,16,512]{2,0,1:T(8,128)}, u32[]{:S(2)}) copy-start(f32[128,16,512]{2,0,1:T(8,128)} %get-tuple-element.175) | copy-start | bytes 12582916 | tf_op jit(solution)/shard_map/while
  393.2 1.9 copy-start.2
  395.2 6.6 %collective-permute-start = (s32[128]{0:T(128)S(1)}, s32[128]{0:T(128)S(1)}, u32[]{:S(2)}, u32[]{:S(2)}) collective-permute-start(s32[128]{0:T(128)S(1)} %get-tuple-element.177), channel_id=1, source_target_pairs={{0,4},{4,8},{8,12},{12,16},{16,20},{20,24},{24,28},{28,32},{32,36}... | collective-permute-start | bytes 1544 | tf_op jit(solution)/shard_map/while/body/eval_jaxpr/ppermute | solution.py:9
  395.2 8.4 %collective-permute-start.1 = (bf16[128,576]{1,0:T(8,128)(2,1)S(1)}, bf16[128,576]{1,0:T(8,128)(2,1)S(1)}, u32[]{:S(2)}, u32[]{:S(2)}) collective-permute-start(bf16[128,576]{1,0:T(8,128)(2,1)S(1)} %get-tuple-element.176), channel_id=1, source_target_pairs={{0,4},{4,8},{8,12},{12,16},{16,20},{20,24},{24,28},{28,32},{32,36}... | collective-permute-start | bytes 442376 | tf_op jit(solution)/shard_map/while/body/eval_jaxpr/ppermute | solution.py:9
  395.2 11.4 %copy-start.1 = (f32[128,16,512]{2,0,1:T(8,128)S(1)}, f32[128,16,512]{2,0,1:T(8,128)}, u32[]{:S(2)}) copy-start(f32[128,16,512]{2,0,1:T(8,128)} %get-tuple-element.175) | copy-start | bytes 12582916 | tf_op jit(solution)/shard_map/while
  408.2 1.9 copy-start.2
  410.2 6.6 %collective-permute-start = (s32[128]{0:T(128)S(1)}, s32[128]{0:T(128)S(1)}, u32[]{:S(2)}, u32[]{:S(2)}) collective-permute-start(s32[128]{0:T(128)S(1)} %get-tuple-element.177), channel_id=1, source_target_pairs={{0,4},{4,8},{8,12},{12,16},{16,20},{20,24},{24,28},{28,32},{32,36}... | collective-permute-start | bytes 1544 | tf_op jit(solution)/shard_map/while/body/eval_jaxpr/ppermute | solution.py:9
  410.2 8.4 %collective-permute-start.1 = (bf16[128,576]{1,0:T(8,128)(2,1)S(1)}, bf16[128,576]{1,0:T(8,128)(2,1)S(1)}, u32[]{:S(2)}, u32[]{:S(2)}) collective-permute-start(bf16[128,576]{1,0:T(8,128)(2,1)S(1)} %get-tuple-element.176), channel_id=1, source_target_pairs={{0,4},{4,8},{8,12},{12,16},{16,20},{20,24},{24,28},{28,32},{32,36}... | collective-permute-start | bytes 442376 | tf_op jit(solution)/shard_map/while/body/eval_jaxpr/ppermute | solution.py:9
  410.2 11.4 %copy-start.1 = (f32[128,16,512]{2,0,1:T(8,128)S(1)}, f32[128,16,512]{2,0,1:T(8,128)}, u32[]{:S(2)}) copy-start(f32[128,16,512]{2,0,1:T(8,128)} %get-tuple-element.175) | copy-start | bytes 12582916 | tf_op jit(solution)/shard_map/while
  423.3 1.9 copy-start.2
  425.2 6.6 %collective-permute-start = (s32[128]{0:T(128)S(1)}, s32[128]{0:T(128)S(1)}, u32[]{:S(2)}, u32[]{:S(2)}) collective-permute-start(s32[128]{0:T(128)S(1)} %get-tuple-element.177), channel_id=1, source_target_pairs={{0,4},{4,8},{8,12},{12,16},{16,20},{20,24},{24,28},{28,32},{32,36}... | collective-permute-start | bytes 1544 | tf_op jit(solution)/shard_map/while/body/eval_jaxpr/ppermute | solution.py:9
  425.2 8.4 %collective-permute-start.1 = (bf16[128,576]{1,0:T(8,128)(2,1)S(1)}, bf16[128,576]{1,0:T(8,128)(2,1)S(1)}, u32[]{:S(2)}, u32[]{:S(2)}) collective-permute-start(bf16[128,576]{1,0:T(8,128)(2,1)S(1)} %get-tuple-element.176), channel_id=1, source_target_pairs={{0,4},{4,8},{8,12},{12,16},{16,20},{20,24},{24,28},{28,32},{32,36}... | collective-permute-start | bytes 442376 | tf_op jit(solution)/shard_map/while/body/eval_jaxpr/ppermute | solution.py:9
  425.2 11.4 %copy-start.1 = (f32[128,16,512]{2,0,1:T(8,128)S(1)}, f32[128,16,512]{2,0,1:T(8,128)}, u32[]{:S(2)}) copy-start(f32[128,16,512]{2,0,1:T(8,128)} %get-tuple-element.175) | copy-start | bytes 12582916 | tf_op jit(solution)/shard_map/while
  438.3 1.9 copy-start.2
  440.2 6.6 %collective-permute-start = (s32[128]{0:T(128)S(1)}, s32[128]{0:T(128)S(1)}, u32[]{:S(2)}, u32[]{:S(2)}) collective-permute-start(s32[128]{0:T(128)S(1)} %get-tuple-element.177), channel_id=1, source_target_pairs={{0,4},{4,8},{8,12},{12,16},{16,20},{20,24},{24,28},{28,32},{32,36}... | collective-permute-start | bytes 1544 | tf_op jit(solution)/shard_map/while/body/eval_jaxpr/ppermute | solution.py:9
  440.2 8.4 %collective-permute-start.1 = (bf16[128,576]{1,0:T(8,128)(2,1)S(1)}, bf16[128,576]{1,0:T(8,128)(2,1)S(1)}, u32[]{:S(2)}, u32[]{:S(2)}) collective-permute-start(bf16[128,576]{1,0:T(8,128)(2,1)S(1)} %get-tuple-element.176), channel_id=1, source_target_pairs={{0,4},{4,8},{8,12},{12,16},{16,20},{20,24},{24,28},{28,32},{32,36}... | collective-permute-start | bytes 442376 | tf_op jit(solution)/shard_map/while/body/eval_jaxpr/ppermute | solution.py:9
  440.2 11.4 %copy-start.1 = (f32[128,16,512]{2,0,1:T(8,128)S(1)}, f32[128,16,512]{2,0,1:T(8,128)}, u32[]{:S(2)}) copy-start(f32[128,16,512]{2,0,1:T(8,128)} %get-tuple-element.175) | copy-start | bytes 12582916 | tf_op jit(solution)/shard_map/while
  453.3 1.9 copy-start.2
  455.2 6.6 %collective-permute-start = (s32[128]{0:T(128)S(1)}, s32[128]{0:T(128)S(1)}, u32[]{:S(2)}, u32[]{:S(2)}) collective-permute-start(s32[128]{0:T(128)S(1)} %get-tuple-element.177), channel_id=1, source_target_pairs={{0,4},{4,8},{8,12},{12,16},{16,20},{20,24},{24,28},{28,32},{32,36}... | collective-permute-start | bytes 1544 | tf_op jit(solution)/shard_map/while/body/eval_jaxpr/ppermute | solution.py:9
  455.2 8.4 %collective-permute-start.1 = (bf16[128,576]{1,0:T(8,128)(2,1)S(1)}, bf16[128,576]{1,0:T(8,128)(2,1)S(1)}, u32[]{:S(2)}, u32[]{:S(2)}) collective-permute-start(bf16[128,576]{1,0:T(8,128)(2,1)S(1)} %get-tuple-element.176), channel_id=1, source_target_pairs={{0,4},{4,8},{8,12},{12,16},{16,20},{20,24},{24,28},{28,32},{32,36}... | collective-permute-start | bytes 442376 | tf_op jit(solution)/shard_map/while/body/eval_jaxpr/ppermute | solution.py:9
  455.2 11.4 %copy-start.1 = (f32[128,16,512]{2,0,1:T(8,128)S(1)}, f32[128,16,512]{2,0,1:T(8,128)}, u32[]{:S(2)}) copy-start(f32[128,16,512]{2,0,1:T(8,128)} %get-tuple-element.175) | copy-start | bytes 12582916 | tf_op jit(solution)/shard_map/while
  468.3 1.9 copy-start.2
  470.2 6.6 %collective-permute-start = (s32[128]{0:T(128)S(1)}, s32[128]{0:T(128)S(1)}, u32[]{:S(2)}, u32[]{:S(2)}) collective-permute-start(s32[128]{0:T(128)S(1)} %get-tuple-element.177), channel_id=1, source_target_pairs={{0,4},{4,8},{8,12},{12,16},{16,20},{20,24},{24,28},{28,32},{32,36}... | collective-permute-start | bytes 1544 | tf_op jit(solution)/shard_map/while/body/eval_jaxpr/ppermute | solution.py:9
  470.2 8.4 %collective-permute-start.1 = (bf16[128,576]{1,0:T(8,128)(2,1)S(1)}, bf16[128,576]{1,0:T(8,128)(2,1)S(1)}, u32[]{:S(2)}, u32[]{:S(2)}) collective-permute-start(bf16[128,576]{1,0:T(8,128)(2,1)S(1)} %get-tuple-element.176), channel_id=1, source_target_pairs={{0,4},{4,8},{8,12},{12,16},{16,20},{20,24},{24,28},{28,32},{32,36}... | collective-permute-start | bytes 442376 | tf_op jit(solution)/shard_map/while/body/eval_jaxpr/ppermute | solution.py:9
  470.2 11.4 %copy-start.1 = (f32[128,16,512]{2,0,1:T(8,128)S(1)}, f32[128,16,512]{2,0,1:T(8,128)}, u32[]{:S(2)}) copy-start(f32[128,16,512]{2,0,1:T(8,128)} %get-tuple-element.175) | copy-start | bytes 12582916 | tf_op jit(solution)/shard_map/while
  483.3 1.9 copy-start.2
  485.2 6.6 %collective-permute-start = (s32[128]{0:T(128)S(1)}, s32[128]{0:T(128)S(1)}, u32[]{:S(2)}, u32[]{:S(2)}) collective-permute-start(s32[128]{0:T(128)S(1)} %get-tuple-element.177), channel_id=1, source_target_pairs={{0,4},{4,8},{8,12},{12,16},{16,20},{20,24},{24,28},{28,32},{32,36}... | collective-permute-start | bytes 1544 | tf_op jit(solution)/shard_map/while/body/eval_jaxpr/ppermute | solution.py:9
  485.2 8.4 %collective-permute-start.1 = (bf16[128,576]{1,0:T(8,128)(2,1)S(1)}, bf16[128,576]{1,0:T(8,128)(2,1)S(1)}, u32[]{:S(2)}, u32[]{:S(2)}) collective-permute-start(bf16[128,576]{1,0:T(8,128)(2,1)S(1)} %get-tuple-element.176), channel_id=1, source_target_pairs={{0,4},{4,8},{8,12},{12,16},{16,20},{20,24},{24,28},{28,32},{32,36}... | collective-permute-start | bytes 442376 | tf_op jit(solution)/shard_map/while/body/eval_jaxpr/ppermute | solution.py:9
  485.2 11.4 %copy-start.1 = (f32[128,16,512]{2,0,1:T(8,128)S(1)}, f32[128,16,512]{2,0,1:T(8,128)}, u32[]{:S(2)}) copy-start(f32[128,16,512]{2,0,1:T(8,128)} %get-tuple-element.175) | copy-start | bytes 12582916 | tf_op jit(solution)/shard_map/while
  498.3 1.9 copy-start.2
  500.2 6.8 %collective-permute-start = (s32[128]{0:T(128)S(1)}, s32[128]{0:T(128)S(1)}, u32[]{:S(2)}, u32[]{:S(2)}) collective-permute-start(s32[128]{0:T(128)S(1)} %get-tuple-element.177), channel_id=1, source_target_pairs={{0,4},{4,8},{8,12},{12,16},{16,20},{20,24},{24,28},{28,32},{32,36}... | collective-permute-start | bytes 1544 | tf_op jit(solution)/shard_map/while/body/eval_jaxpr/ppermute | solution.py:9
  500.2 8.4 %collective-permute-start.1 = (bf16[128,576]{1,0:T(8,128)(2,1)S(1)}, bf16[128,576]{1,0:T(8,128)(2,1)S(1)}, u32[]{:S(2)}, u32[]{:S(2)}) collective-permute-start(bf16[128,576]{1,0:T(8,128)(2,1)S(1)} %get-tuple-element.176), channel_id=1, source_target_pairs={{0,4},{4,8},{8,12},{12,16},{16,20},{20,24},{24,28},{28,32},{32,36}... | collective-permute-start | bytes 442376 | tf_op jit(solution)/shard_map/while/body/eval_jaxpr/ppermute | solution.py:9
  500.2 11.4 %copy-start.1 = (f32[128,16,512]{2,0,1:T(8,128)S(1)}, f32[128,16,512]{2,0,1:T(8,128)}, u32[]{:S(2)}) copy-start(f32[128,16,512]{2,0,1:T(8,128)} %get-tuple-element.175) | copy-start | bytes 12582916 | tf_op jit(solution)/shard_map/while
  513.3 1.9 copy-start.2
  515.2 6.9 %collective-permute-start = (s32[128]{0:T(128)S(1)}, s32[128]{0:T(128)S(1)}, u32[]{:S(2)}, u32[]{:S(2)}) collective-permute-start(s32[128]{0:T(128)S(1)} %get-tuple-element.177), channel_id=1, source_target_pairs={{0,4},{4,8},{8,12},{12,16},{16,20},{20,24},{24,28},{28,32},{32,36}... | collective-permute-start | bytes 1544 | tf_op jit(solution)/shard_map/while/body/eval_jaxpr/ppermute | solution.py:9
  515.2 9.4 %collective-permute-start.1 = (bf16[128,576]{1,0:T(8,128)(2,1)S(1)}, bf16[128,576]{1,0:T(8,128)(2,1)S(1)}, u32[]{:S(2)}, u32[]{:S(2)}) collective-permute-start(bf16[128,576]{1,0:T(8,128)(2,1)S(1)} %get-tuple-element.176), channel_id=1, source_target_pairs={{0,4},{4,8},{8,12},{12,16},{16,20},{20,24},{24,28},{28,32},{32,36}... | collective-permute-start | bytes 442376 | tf_op jit(solution)/shard_map/while/body/eval_jaxpr/ppermute | solution.py:9
  515.2 12.4 %copy-start.1 = (f32[128,16,512]{2,0,1:T(8,128)S(1)}, f32[128,16,512]{2,0,1:T(8,128)}, u32[]{:S(2)}) copy-start(f32[128,16,512]{2,0,1:T(8,128)} %get-tuple-element.175) | copy-start | bytes 12582916 | tf_op jit(solution)/shard_map/while
  531.3 6.6 %collective-permute-start = (s32[128]{0:T(128)S(1)}, s32[128]{0:T(128)S(1)}, u32[]{:S(2)}, u32[]{:S(2)}) collective-permute-start(s32[128]{0:T(128)S(1)} %get-tuple-element.177), channel_id=1, source_target_pairs={{0,4},{4,8},{8,12},{12,16},{16,20},{20,24},{24,28},{28,32},{32,36}... | collective-permute-start | bytes 1544 | tf_op jit(solution)/shard_map/while/body/eval_jaxpr/ppermute | solution.py:9
  531.3 10.0 %collective-permute-start.1 = (bf16[128,576]{1,0:T(8,128)(2,1)S(1)}, bf16[128,576]{1,0:T(8,128)(2,1)S(1)}, u32[]{:S(2)}, u32[]{:S(2)}) collective-permute-start(bf16[128,576]{1,0:T(8,128)(2,1)S(1)} %get-tuple-element.176), channel_id=1, source_target_pairs={{0,4},{4,8},{8,12},{12,16},{16,20},{20,24},{24,28},{28,32},{32,36}... | collective-permute-start | bytes 442376 | tf_op jit(solution)/shard_map/while/body/eval_jaxpr/ppermute | solution.py:9
  531.3 13.0 %copy-start.1 = (f32[128,16,512]{2,0,1:T(8,128)S(1)}, f32[128,16,512]{2,0,1:T(8,128)}, u32[]{:S(2)}) copy-start(f32[128,16,512]{2,0,1:T(8,128)} %get-tuple-element.175) | copy-start | bytes 12582916 | tf_op jit(solution)/shard_map/while
  547.9 6.6 %collective-permute-start = (s32[128]{0:T(128)S(1)}, s32[128]{0:T(128)S(1)}, u32[]{:S(2)}, u32[]{:S(2)}) collective-permute-start(s32[128]{0:T(128)S(1)} %get-tuple-element.177), channel_id=1, source_target_pairs={{0,4},{4,8},{8,12},{12,16},{16,20},{20,24},{24,28},{28,32},{32,36}... | collective-permute-start | bytes 1544 | tf_op jit(solution)/shard_map/while/body/eval_jaxpr/ppermute | solution.py:9
  547.9 9.2 %collective-permute-start.1 = (bf16[128,576]{1,0:T(8,128)(2,1)S(1)}, bf16[128,576]{1,0:T(8,128)(2,1)S(1)}, u32[]{:S(2)}, u32[]{:S(2)}) collective-permute-start(bf16[128,576]{1,0:T(8,128)(2,1)S(1)} %get-tuple-element.176), channel_id=1, source_target_pairs={{0,4},{4,8},{8,12},{12,16},{16,20},{20,24},{24,28},{28,32},{32,36}... | collective-permute-start | bytes 442376 | tf_op jit(solution)/shard_map/while/body/eval_jaxpr/ppermute | solution.py:9
  547.9 12.1 %copy-start.1 = (f32[128,16,512]{2,0,1:T(8,128)S(1)}, f32[128,16,512]{2,0,1:T(8,128)}, u32[]{:S(2)}) copy-start(f32[128,16,512]{2,0,1:T(8,128)} %get-tuple-element.175) | copy-start | bytes 12582916 | tf_op jit(solution)/shard_map/while
  (3 other events, 5.8 us)
Sparse Core Ops, SparseCore 0:
  578.9 57.2 reduce-scatter.1
